TPU v7x, 512 devices: a whole 4x4x16 slice. The times are simulated.
512 devices in a mesh: tm: 32 (over z, core), bat: 16 (over y, x).
Axes of the slice: x: 4, y: 4, z: 16, core: 2. Of those that a mesh axis runs over, the one named last changes fastest.
Arguments:
- power0: float32 [512, 6144], P('tm', 'bat'), may hold values from -0.5 to 0.5
- charge0: float32 [512, 6144], P('tm', 'bat'), may hold values from 0 to 1
- dyn_dual0: float32 [512, 6144], P('tm', 'bat'), may hold values from -3 to 3
- feeder_dual0: float32 [512, 3072], P(('tm', 'bat')), may hold values from 0 to 0.5
- price: float32 [512, 6144], P('tm', 'bat'), may hold values from -12 to 12
- inflow: float32 [512, 6144], P('tm', 'bat'), may hold values from -1.5 to 1.5
- power_limit: float32 [6144], P('bat'), may hold values from 0.5 to 6
- capacity: float32 [6144], P('bat'), may hold values from 0.5 to 8
- feeder_limit: float32 [3072], replicated, may hold values from 0 to 1
- block_values: float32 [72, 128, 128], replicated, may hold values from -0.3125 to 0.3125
- block_cols: int32 [72], replicated, may hold values from 0 to 47, as said below
- block_offsets: int32 [25], replicated, may hold values from 0 to 72, as said below
Outputs:
- power: float32 [512, 6144], P('tm', 'bat')
- charge: float32 [512, 6144], P('tm', 'bat')
- dyn_dual: float32 [512, 6144], P('tm', 'bat')
- feeder_dual: float32 [512, 3072], P(('tm', 'bat'))
Inputs may be any that keep to these rules, and one draw needn't show every extreme that they name: `block_cols`: every battery block 0 to 47 appears at least once. block_offsets[0] = 0, strictly rising, block_offsets[24] = 72.
All inputs are finite; a program needn't handle non-finite values.
Results may differ from a plain program's by a relative error of at most 0.0001.
Values sent between devices are 32-bit elements; how exact they have to be, the bound alone decides.
No kernel may reach another device: no remote copies, remote signals or barrier semaphores. Data moves between devices by JAX's collectives and lax.ppermute only.
A program may use at most 64 MiB of HBM per device.

v0:
```python
import jax
import jax.numpy as jnp
from jax import lax
from jax.sharding import PartitionSpec as P

ITERS = 4
HIGH = lax.Precision.HIGHEST
ETA_STEP = 0.4
EPS_NORM = 1e-06


def shifted(block, axis, distance):
    devices = range(lax.axis_size(axis))
    route = [(i - distance, i) for i in devices if i - distance in devices]
    return lax.ppermute(block, axis, route)


def row_table(block_offsets, count):
    index_all = jnp.arange(count, dtype=jnp.int32)
    row_of = jnp.sum((index_all[:, None] >= block_offsets[None, 1:-1]).astype(jnp.int32), axis=1)
    feed_count = block_offsets.shape[0] - 1
    return (row_of[:, None] == jnp.arange(feed_count, dtype=jnp.int32)[None, :]).astype(jnp.float32)


def feeder_apply(field, block_values, rows_tab, cols_tab):
    count_rows = field.shape[0]
    blk = block_values.shape[1]
    blocks = field.reshape(count_rows, -1, blk)
    picked = jnp.einsum("rnk,jn->rjk", blocks, cols_tab, precision=HIGH)
    partial_rows = jnp.einsum("rjk,jmk->rjm", picked, block_values, precision=HIGH)
    summed = jnp.einsum("rjm,jf->rfm", partial_rows, rows_tab, precision=HIGH)
    return summed.reshape(count_rows, -1)


def feeder_adjoint(duals, block_values, rows_tab, cols_tab):
    count_rows = duals.shape[0]
    blk = block_values.shape[1]
    blocks = duals.reshape(count_rows, -1, blk)
    chosen = jnp.einsum("rfm,jf->rjm", blocks, rows_tab, precision=HIGH)
    pushed = jnp.einsum("rjm,jmk->rjk", chosen, block_values, precision=HIGH)
    spread = jnp.einsum("rjk,jn->rnk", pushed, cols_tab, precision=HIGH)
    return spread.reshape(count_rows, -1)


def shards(
    power0,
    charge0,
    dyn_dual0,
    feeder_dual0,
    price,
    inflow,
    power_limit,
    capacity,
    feeder_limit,
    block_values,
    block_cols,
    block_offsets,
):
    blk = block_values.shape[1]
    rows_tab = row_table(block_offsets, block_values.shape[0])
    local_batteries = power0.shape[1]
    local_blocks = local_batteries // blk
    first_block = lax.axis_index("bat") * local_blocks
    inside = (block_cols >= first_block) & (block_cols < first_block + local_blocks)
    local_cols = jnp.clip(block_cols - first_block, 0, local_blocks - 1)
    local_tab = (
        (local_cols[:, None] == jnp.arange(local_blocks, dtype=jnp.int32)[None, :])
        & inside[:, None]
    ).astype(jnp.float32)

    def couple_backward(duals):
        return feeder_adjoint(
            lax.all_gather(duals, "bat", axis=0, tiled=True), block_values, rows_tab, local_tab
        )

    power, charge, dyn_dual, feeder_dual = (power0, charge0, dyn_dual0, feeder_dual0)
    weight = jnp.asarray(1.0, dtype=jnp.float32)
    pushed = couple_backward(feeder_dual)
    limit_row = power_limit[None, :]
    for iteration in range(ITERS):
        step_primal = ETA_STEP / weight
        step_dual = ETA_STEP * weight
        following = shifted(dyn_dual[:1], "tm", -1)
        dual_next = jnp.concatenate([dyn_dual[1:], following], axis=0)
        power_new = jnp.clip(
            power - step_primal * (price - dyn_dual + pushed), -limit_row, limit_row
        )
        charge_new = jnp.clip(charge - step_primal * (dyn_dual - dual_next), 0.0, capacity[None, :])
        power_bar = 2.0 * power_new - power
        charge_bar = 2.0 * charge_new - charge
        last_iteration = iteration + 1 == ITERS
        if not last_iteration:
            move_power = power_new - power
            move_charge = charge_new - charge
            primal_local = jnp.sum(move_power * move_power + move_charge * move_charge)
            primal_sq = lax.psum(primal_local, ("tm", "bat"))
        coupled = lax.psum_scatter(
            feeder_apply(power_bar, block_values, rows_tab, local_tab),
            "bat",
            scatter_dimension=0,
            tiled=True,
        )
        preceding = shifted(charge_bar[-1:], "tm", 1)
        charge_prev = jnp.concatenate([preceding, charge_bar[:-1]], axis=0)
        dyn_new = dyn_dual + step_dual * (charge_bar - charge_prev - power_bar - inflow)
        feeder_new = jnp.maximum(0.0, feeder_dual + step_dual * (coupled - feeder_limit[None, :]))
        if not last_iteration:
            move_dyn = dyn_new - dyn_dual
            move_feed = feeder_new - feeder_dual
            dual_local = jnp.sum(move_dyn * move_dyn) + jnp.sum(move_feed * move_feed)
            dual_sq = lax.psum(dual_local, ("tm", "bat"))
            weight = jnp.sqrt(weight * jnp.sqrt((dual_sq + EPS_NORM) / (primal_sq + EPS_NORM)))
            pushed = couple_backward(feeder_new)
        power, charge, dyn_dual, feeder_dual = (power_new, charge_new, dyn_new, feeder_new)
    return (power, charge, dyn_dual, feeder_dual)


def solution(mesh):
    return jax.shard_map(
        shards,
        mesh=mesh,
        in_specs=(
            P("tm", "bat"),
            P("tm", "bat"),
            P("tm", "bat"),
            P(("tm", "bat"), None),
            P("tm", "bat"),
            P("tm", "bat"),
            P("bat"),
            P("bat"),
            P(),
            P(),
            P(),
            P(),
        ),
        out_specs=(P("tm", "bat"), P("tm", "bat"), P("tm", "bat"), P(("tm", "bat"), None)),
        check_vma=False,
    )
```

profile of v0, /device:TPU:2, one launch (start us, length us, event | category | flops | bytes accessed | tf_op | source)
XLA Modules:
  0.0 976.7 jit_solution(11067665464385182962)
XLA Ops:
  8.0 1.3 collective-permute-start
  11.4 26.6 %all-gather = f32[16,1,3072]{2,1,0:T(1,128)S(1)} all-gather(f32[1,1,3072]{2,1,0:T(1,128)} %bitcast.181), channel_id=1, replica_groups=mesh['tm'=32,'bat'=16] {'bat'}, dimensions={0}, use_global_device_ids=true | all-gather | bytes 208896 | tf_op jit(solution)/shard_map/all_gather | solution.py:73
  38.5 5.8 convolution_bitcast_fusion.15
  45.5 1.3 collective-permute-start.1
  48.7 9.2 convolution_bitcast_fusion.14
  59.2 1.3 dynamic-slice
  60.5 1.3 collective-permute-start.2
  61.8 115.7 %all-reduce.12.cloned.1.call-done = f32[16,3072]{1,0:T(8,128)} async-done(((f32[16,3072]{1,0:T(8,128)}), f32[16,3072]{1,0:T(8,128)}) %all-reduce.12.cloned.1.call-update) | async-done | bytes 196624
  177.5 2.2 multiply_reduce_fusion.5
  179.7 22.0 %all-gather.1 = f32[16,1,3072]{2,1,0:T(1,128)S(1)} all-gather(f32[1,1,3072]{2,1,0:T(1,128)S(1)} %bitcast.179), channel_id=1, replica_groups=mesh['tm'=32,'bat'=16] {'bat'}, dimensions={0}, use_global_device_ids=true | all-gather | bytes 208896 | tf_op jit(solution)/shard_map/all_gather | solution.py:73
  202.1 5.8 convolution_bitcast_fusion.13
  209.7 103.0 %all-reduce.6 = (f32[]{:T(128)}, f32[]{:T(128)}) all-reduce(f32[]{:T(128)S(6)} %add.99, f32[]{:T(128)} %get-tuple-element.31), channel_id=1, replica_groups=mesh['tm'=32,'bat'=16] {'tm','bat'}, use_global_device_ids=true, to_apply=%region_4.5 | all-reduce | flops 2 | bytes 16 | tf_op jit(solution)/shard_map/psum | solution.py:111
  314.8 1.9 collective-permute-start.3
  318.5 9.2 convolution_bitcast_fusion.12
  329.0 1.3 collective-permute-start.4
  330.3 110.9 %all-reduce.14.cloned.1.call-done = f32[16,3072]{1,0:T(8,128)} async-done(((f32[16,3072]{1,0:T(8,128)}), f32[16,3072]{1,0:T(8,128)}) %all-reduce.14.cloned.1.call-update) | async-done | bytes 196624
  441.1 2.2 multiply_reduce_fusion.4
  443.3 22.0 %all-gather.2 = f32[16,1,3072]{2,1,0:T(1,128)S(1)} all-gather(f32[1,1,3072]{2,1,0:T(1,128)S(1)} %bitcast.178), channel_id=1, replica_groups=mesh['tm'=32,'bat'=16] {'bat'}, dimensions={0}, use_global_device_ids=true | all-gather | bytes 208896 | tf_op jit(solution)/shard_map/all_gather | solution.py:73
  465.7 5.8 convolution_bitcast_fusion.11
  473.3 103.0 %all-reduce.5 = (f32[]{:T(128)}, f32[]{:T(128)}) all-reduce(f32[]{:T(128)S(6)} %add.106, f32[]{:T(128)} %get-tuple-element.23), channel_id=1, replica_groups=mesh['tm'=32,'bat'=16] {'tm','bat'}, use_global_device_ids=true, to_apply=%region_10.11 | all-reduce | flops 2 | bytes 16 | tf_op jit(solution)/shard_map/psum | solution.py:111
  578.4 1.7 collective-permute-start.5
  582.1 9.2 convolution_bitcast_fusion.10
  592.5 1.3 collective-permute-start.6
  593.8 110.9 %all-reduce.16.cloned.1.call-done = f32[16,3072]{1,0:T(8,128)} async-done(((f32[16,3072]{1,0:T(8,128)}), f32[16,3072]{1,0:T(8,128)}) %all-reduce.16.cloned.1.call-update) | async-done | bytes 196624
  704.7 2.2 multiply_reduce_fusion.3
  706.9 22.2 %all-gather.3 = f32[16,1,3072]{2,1,0:T(1,128)S(1)} all-gather(f32[1,1,3072]{2,1,0:T(1,128)S(1)} %bitcast.180), channel_id=1, replica_groups=mesh['tm'=32,'bat'=16] {'bat'}, dimensions={0}, use_global_device_ids=true | all-gather | bytes 208896 | tf_op jit(solution)/shard_map/all_gather | solution.py:73
  729.5 5.8 convolution_bitcast_fusion.9
  736.7 103.0 %all-reduce.4 = (f32[]{:T(128)}, f32[]{:T(128)}) all-reduce(f32[]{:T(128)S(6)} %add.113, f32[]{:T(128)} %get-tuple-element.15), channel_id=1, replica_groups=mesh['tm'=32,'bat'=16] {'tm','bat'}, use_global_device_ids=true, to_apply=%region_16.17 | all-reduce | flops 2 | bytes 16 | tf_op jit(solution)/shard_map/psum | solution.py:111
  841.8 1.7 collective-permute-start.7
  845.4 9.2 convolution_bitcast_fusion.8
  855.8 112.2 %all-reduce.18.cloned.1.call-done = f32[16,3072]{1,0:T(8,128)} async-done(((f32[16,3072]{1,0:T(8,128)}), f32[16,3072]{1,0:T(8,128)}) %all-reduce.18.cloned.1.call-update) | async-done | bytes 196624
  968.0 2.1 fusion.92
  (87 shorter events, 20.9 us)
Async XLA Ops:
  7.2 37.6 %copy-start.2 = (f32[16,384]{1,0:T(8,128)S(1)}, f32[16,384]{1,0:T(8,128)}, u32[]{:S(2)}) copy-start(f32[16,384]{1,0:T(8,128)} %param.14) | copy-start | bytes 73732
  7.2 37.6 %copy-start.6 = (f32[384]{0:T(512)S(1)}, f32[384]{0:T(512)}, u32[]{:S(2)}) copy-start(f32[384]{0:T(512)} %param.18) | copy-start | bytes 4612
  7.2 37.6 %copy-start.4 = (f32[16,384]{1,0:T(8,128)S(1)}, f32[16,384]{1,0:T(8,128)}, u32[]{:S(2)}) copy-start(f32[16,384]{1,0:T(8,128)} %param.12) | copy-start | bytes 73732
  7.2 37.6 %copy-start.5 = (f32[16,384]{1,0:T(8,128)S(1)}, f32[16,384]{1,0:T(8,128)}, u32[]{:S(2)}) copy-start(f32[16,384]{1,0:T(8,128)} %param.13) | copy-start | bytes 73732
  7.2 37.6 %copy-start.1 = (f32[16,384]{1,0:T(8,128)S(1)}, f32[16,384]{1,0:T(8,128)}, u32[]{:S(2)}) copy-start(f32[16,384]{1,0:T(8,128)} %param.16) | copy-start | bytes 73732
  7.2 37.6 %copy-start.8 = (f32[384]{0:T(512)S(1)}, f32[384]{0:T(512)}, u32[]{:S(2)}) copy-start(f32[384]{0:T(512)} %param.19) | copy-start | bytes 4612
  7.2 40.4 %copy-start = (f32[16,384]{1,0:T(8,128)S(1)}, f32[16,384]{1,0:T(8,128)}, u32[]{:S(2)}) copy-start(f32[16,384]{1,0:T(8,128)} %param.17) | copy-start | bytes 73732
  7.2 170.3 %all-reduce.12.cloned.1.call-start = ((), (), s32[]{:S(2)}) async-start(), calls=%async_computation | async-start | bytes 393216
  8.0 36.8 %collective-permute-start = (f32[1,384]{1,0:T(1,128)S(1)}, f32[1,384]{1,0:T(1,128)S(1)}, u32[]{:S(2)}, u32[]{:S(2)}) collective-permute-start(f32[1,384]{1,0:T(1,128)S(1)} %slice.53), channel_id=1, source_target_pairs={{16,0},{32,16},{48,32},{64,48},{80,64},{96,80},{112,96},{128,112},... | collective-permute-start | bytes 4616 | tf_op jit(solution)/shard_map/ppermute | solution.py:15
  44.3 133.2 %copy-start.3 = (f32[3072]{0:T(1024)S(1)}, f32[3072]{0:T(1024)}, u32[]{:S(2)}) copy-start(f32[3072]{0:T(1024)} %param.20) | copy-start | bytes 36868
  44.3 133.2 %copy-start.7 = (f32[1,3072]{1,0:T(1,128)S(1)}, f32[1,3072]{1,0:T(1,128)}, u32[]{:S(2)}) copy-start(f32[1,3072]{1,0:T(1,128)} %param.15) | copy-start | bytes 36868
  45.5 2.1 collective-permute-start.1
  59.1 382.0 %all-reduce.14.cloned.1.call-start = ((), (), s32[]{:S(2)}) async-start(), calls=%async_computation.1 | async-start | bytes 393216
  60.5 253.7 %collective-permute-start.2 = (f32[1,384]{1,0:T(1,128)S(1)}, f32[1,384]{1,0:T(1,128)S(1)}, u32[]{:S(2)}, u32[]{:S(2)}) collective-permute-start(f32[1,384]{1,0:T(1,128)S(1)} %slice.71), channel_id=1, source_target_pairs={{16,0},{32,16},{48,32},{64,48},{80,64},{96,80},{112,96},{128,112},... | collective-permute-start | bytes 4616 | tf_op jit(solution)/shard_map/ppermute | solution.py:15
  314.8 2.5 collective-permute-start.3
  328.9 375.8 %all-reduce.16.cloned.1.call-start = ((), (), s32[]{:S(2)}) async-start(), calls=%async_computation.2 | async-start | bytes 393216
  329.0 248.8 %collective-permute-start.4 = (f32[1,384]{1,0:T(1,128)S(1)}, f32[1,384]{1,0:T(1,128)S(1)}, u32[]{:S(2)}, u32[]{:S(2)}) collective-permute-start(f32[1,384]{1,0:T(1,128)S(1)} %slice.75), channel_id=1, source_target_pairs={{16,0},{32,16},{48,32},{64,48},{80,64},{96,80},{112,96},{128,112},... | collective-permute-start | bytes 4616 | tf_op jit(solution)/shard_map/ppermute | solution.py:15
  578.4 2.5 collective-permute-start.5
  592.5 375.6 %all-reduce.18.cloned.1.call-start = ((), (), s32[]{:S(2)}) async-start(), calls=%async_computation.3 | async-start | bytes 393216
  592.5 248.6 %collective-permute-start.6 = (f32[1,384]{1,0:T(1,128)S(1)}, f32[1,384]{1,0:T(1,128)S(1)}, u32[]{:S(2)}, u32[]{:S(2)}) collective-permute-start(f32[1,384]{1,0:T(1,128)S(1)} %slice.79), channel_id=1, source_target_pairs={{16,0},{32,16},{48,32},{64,48},{80,64},{96,80},{112,96},{128,112},... | collective-permute-start | bytes 4616 | tf_op jit(solution)/shard_map/ppermute | solution.py:15
  841.8 2.5 collective-permute-start.7
Sparse Core Ops, SparseCore 0:
  59.2 118.2 all-reduce.11
  329.0 112.0 all-reduce.13
  592.6 112.0 all-reduce.15
  855.9 112.0 all-reduce.17
where the time goes:
time: 978 us; the launch traced here: 977 us
  waiting for transfers between devices  452 us (46%)
  blocking collectives  402 us (41%)
  matrix products  67.2 us (7%)
  between operations  22.5 us (2%)
  other arithmetic  15.1 us (2%)
  starting transfers between devices  12 us (1%)
    unnamed x8, waiting for transfers between devices  450 us
    psum x3, blocking collectives, shards(): dual_sq = lax.psum(dual_local, ('tm', 'bat'))  309 us
    all_gather x4, blocking collectives, couple_backward(): lax.all_gather(duals, 'bat', axis=0, tiled=True)  92.9 us
    dot_general x4, matrix products, feeder_apply(): jnp.einsum('rjk,jmk->rjm', picked, block_values, precision=HIGH)  36.7 us
    dot_general x4, matrix products, feeder_adjoint(): pushed = jnp.einsum('rjm,jmk->rjk', chosen, block_values, precision=HIGH)  23.3 us
  transfers between devices with their start and end apart: 12, of which 8 were waited for; matrix products, arithmetic and copies ran while one was open for 4% of the time, Pallas kernels for 0%

commit v1 on v0

--- a/solution.py
+++ b/solution.py
@@ -70,7 +70,12 @@
 
     def couple_backward(duals):
         return feeder_adjoint(
-            lax.all_gather(duals, "bat", axis=0, tiled=True), block_values, rows_tab, local_tab
+            jnp.concatenate(
+                lax.all_to_all(jnp.stack([duals] * lax.axis_size("bat")), "bat", 0, 0), axis=0
+            ),
+            block_values,
+            rows_tab,
+            local_tab,
         )
 
     power, charge, dyn_dual, feeder_dual = (power0, charge0, dyn_dual0, feeder_dual0)

time: 978 us -> 930 us (0.951)
  blocking collectives: 402 us -> 313 us
  starting transfers between devices: 12 us -> 39 us
    all_gather x4 -> x0, blocking collectives: 92.9 us -> none  [couple_backward(): lax.all_gather(duals, 'bat', axis=0, tiled=True)]
    all_to_all x0 -> x4, starting transfers between devices: none -> 27.2 us  [couple_backward(): lax.all_to_all(jnp.stack([duals] * lax.axis_size('bat')), 'bat', 0, 0)]
  transfers between devices with their start and end apart: 12 -> 16, of which waited for: 8 -> 9; matrix products, arithmetic and copies ran while one was open for 4% -> 4% of each run, Pallas kernels for 0% -> 0%
where the time goes in v1:
time: 930 us; the launch traced here: 928 us
  waiting for transfers between devices  460 us (49%)
  blocking collectives  313 us (34%)
  matrix products  67.2 us (7%)
  starting transfers between devices  39 us (4%)
  between operations  22.5 us (2%)
  other arithmetic  15.8 us (2%)
  local copies, waits for them, and re-layouts  10.3 us (1%)
    unnamed x8, waiting for transfers between devices  452 us
    psum x3, blocking collectives, shards(): dual_sq = lax.psum(dual_local, ('tm', 'bat'))  313 us
    dot_general x4, matrix products, feeder_apply(): jnp.einsum('rjk,jmk->rjm', picked, block_values, precision=HIGH)  36.7 us
    all_to_all x4, starting transfers between devices, couple_backward(): lax.all_to_all(jnp.stack([duals] * lax.axis_size('bat')), 'bat', 0, 0)  27.2 us
    dot_general x4, matrix products, feeder_adjoint(): pushed = jnp.einsum('rjm,jmk->rjk', chosen, block_values, precision=HIGH)  23.3 us
  transfers between devices with their start and end apart: 16, of which 9 were waited for; matrix products, arithmetic and copies ran while one was open for 4% of the time, Pallas kernels for 0%

profile of v1, /device:TPU:2, one launch (start us, length us, event | category | flops | bytes accessed | tf_op | source)
XLA Modules:
  0.0 928.1 jit_solution(6738354166904598073)
XLA Ops:
  7.2 1.5 stack.8
  8.8 9.2 all-to-all-start
  23.6 1.4 all-to-all-done
  25.5 5.8 convolution_bitcast_fusion.15
  32.5 1.6 collective-permute-start.1
  36.0 9.2 convolution_bitcast_fusion.14
  47.7 118.1 %all-reduce.12.cloned.1.call-done = f32[16,3072]{1,0:T(8,128)} async-done(((f32[16,3072]{1,0:T(8,128)}), f32[16,3072]{1,0:T(8,128)}) %all-reduce.12.cloned.1.call-update) | async-done | bytes 196624
  165.8 2.2 multiply_reduce_fusion.5
  168.7 5.8 all-to-all-start.1
  174.5 1.3 collective-permute-start.2
  177.1 105.4 %all-reduce.6 = (f32[]{:T(128)}, f32[]{:T(128)}) all-reduce(f32[]{:T(128)S(6)} %add.99, f32[]{:T(128)} %get-tuple-element.31), channel_id=1, replica_groups=mesh['tm'=32,'bat'=16] {'tm','bat'}, use_global_device_ids=true, to_apply=%region_4.5 | all-reduce | flops 2 | bytes 16 | tf_op jit(solution)/shard_map/psum | solution.py:116
  284.4 5.8 convolution_bitcast_fusion.13
  291.3 1.9 collective-permute-start.3
  295.0 9.2 convolution_bitcast_fusion.12
  305.4 113.0 %all-reduce.14.cloned.1.call-done = f32[16,3072]{1,0:T(8,128)} async-done(((f32[16,3072]{1,0:T(8,128)}), f32[16,3072]{1,0:T(8,128)}) %all-reduce.14.cloned.1.call-update) | async-done | bytes 196624
  418.3 2.2 multiply_reduce_fusion.4
  421.3 5.8 all-to-all-start.2
  427.1 1.3 collective-permute-start.4
  429.7 105.4 %all-reduce.5 = (f32[]{:T(128)}, f32[]{:T(128)}) all-reduce(f32[]{:T(128)S(6)} %add.106, f32[]{:T(128)} %get-tuple-element.23), channel_id=1, replica_groups=mesh['tm'=32,'bat'=16] {'tm','bat'}, use_global_device_ids=true, to_apply=%region_10.11 | all-reduce | flops 2 | bytes 16 | tf_op jit(solution)/shard_map/psum | solution.py:116
  537.0 5.8 convolution_bitcast_fusion.11
  543.9 1.7 collective-permute-start.5
  547.5 9.2 convolution_bitcast_fusion.10
  558.0 1.3 collective-permute-start.6
  559.3 111.6 %all-reduce.16.cloned.1.call-done = f32[16,3072]{1,0:T(8,128)} async-done(((f32[16,3072]{1,0:T(8,128)}), f32[16,3072]{1,0:T(8,128)}) %all-reduce.16.cloned.1.call-update) | async-done | bytes 196624
  670.9 2.2 multiply_reduce_fusion.3
  674.4 102.2 %all-reduce.4 = (f32[]{:T(128)}, f32[]{:T(128)}) all-reduce(f32[]{:T(128)S(6)} %add.113, f32[]{:T(128)} %get-tuple-element.15), channel_id=1, replica_groups=mesh['tm'=32,'bat'=16] {'tm','bat'}, use_global_device_ids=true, to_apply=%region_16.17 | all-reduce | flops 2 | bytes 16 | tf_op jit(solution)/shard_map/psum | solution.py:116
  778.8 6.5 all-to-all-start.3
  787.2 5.1 all-to-all-done.3
  792.8 5.8 convolution_bitcast_fusion.9
  800.2 9.2 convolution_bitcast_fusion.8
  810.6 108.8 %all-reduce.18.cloned.1.call-done = f32[16,3072]{1,0:T(8,128)} async-done(((f32[16,3072]{1,0:T(8,128)}), f32[16,3072]{1,0:T(8,128)}) %all-reduce.18.cloned.1.call-update) | async-done | bytes 196624
  919.4 2.1 fusion.92
  (95 shorter events, 28.2 us)
Async XLA Ops:
  7.2 24.6 %copy-start.2 = (f32[16,384]{1,0:T(8,128)S(1)}, f32[16,384]{1,0:T(8,128)}, u32[]{:S(2)}) copy-start(f32[16,384]{1,0:T(8,128)} %param.14) | copy-start | bytes 73732
  7.2 24.6 %copy-start.6 = (f32[384]{0:T(512)S(1)}, f32[384]{0:T(512)}, u32[]{:S(2)}) copy-start(f32[384]{0:T(512)} %param.18) | copy-start | bytes 4612
  7.2 24.6 %copy-start.4 = (f32[16,384]{1,0:T(8,128)S(1)}, f32[16,384]{1,0:T(8,128)}, u32[]{:S(2)}) copy-start(f32[16,384]{1,0:T(8,128)} %param.12) | copy-start | bytes 73732
  7.2 24.6 %copy-start.5 = (f32[16,384]{1,0:T(8,128)S(1)}, f32[16,384]{1,0:T(8,128)}, u32[]{:S(2)}) copy-start(f32[16,384]{1,0:T(8,128)} %param.13) | copy-start | bytes 73732
  7.2 24.6 %copy-start.1 = (f32[16,384]{1,0:T(8,128)S(1)}, f32[16,384]{1,0:T(8,128)}, u32[]{:S(2)}) copy-start(f32[16,384]{1,0:T(8,128)} %param.16) | copy-start | bytes 73732
  7.2 24.6 %copy-start.8 = (f32[384]{0:T(512)S(1)}, f32[384]{0:T(512)}, u32[]{:S(2)}) copy-start(f32[384]{0:T(512)} %param.19) | copy-start | bytes 4612
  7.2 27.7 %copy-start = (f32[16,384]{1,0:T(8,128)S(1)}, f32[16,384]{1,0:T(8,128)}, u32[]{:S(2)}) copy-start(f32[16,384]{1,0:T(8,128)} %param.17) | copy-start | bytes 73732
  8.8 16.3 %all-to-all-start = ((f32[16,1,3072]{2,1,0:T(1,128)}), f32[16,1,3072]{2,1,0:T(1,128)S(1)}, u32[]{:S(2)}, u32[]{:S(2)}) async-start(f32[16,1,3072]{2,1,0:T(1,128)} %stack.8), calls=%async_computation | async-start | bytes 393216 | tf_op jit(solution)/shard_map/all_to_all | solution.py:74
  18.0 147.8 %all-reduce.12.cloned.1.call-start = ((), (), s32[]{:S(2)}) async-start(), calls=%async_computation.4 | async-start | bytes 393216
  18.7 13.1 %collective-permute-start = (f32[1,384]{1,0:T(1,128)S(1)}, f32[1,384]{1,0:T(1,128)S(1)}, u32[]{:S(2)}, u32[]{:S(2)}) collective-permute-start(f32[1,384]{1,0:T(1,128)S(1)} %slice.53), channel_id=1, source_target_pairs={{16,0},{32,16},{48,32},{64,48},{80,64},{96,80},{112,96},{128,112},... | collective-permute-start | bytes 4616 | tf_op jit(solution)/shard_map/ppermute | solution.py:15
  31.3 134.4 %copy-start.3 = (f32[3072]{0:T(1024)S(1)}, f32[3072]{0:T(1024)}, u32[]{:S(2)}) copy-start(f32[3072]{0:T(1024)} %param.20) | copy-start | bytes 36868
  31.3 134.4 %copy-start.7 = (f32[1,3072]{1,0:T(1,128)S(1)}, f32[1,3072]{1,0:T(1,128)}, u32[]{:S(2)}) copy-start(f32[1,3072]{1,0:T(1,128)} %param.15) | copy-start | bytes 36868
  32.5 2.4 collective-permute-start.1
  168.7 115.3 %all-to-all-start.1 = ((f32[16,1,3072]{2,1,0:T(1,128)}), f32[16,1,3072]{2,1,0:T(1,128)S(1)}, u32[]{:S(2)}, u32[]{:S(2)}) async-start(f32[16,1,3072]{2,1,0:T(1,128)} %stack.9), calls=%async_computation.1 | async-start | bytes 393216 | tf_op jit(solution)/shard_map/all_to_all | solution.py:74
  174.5 243.9 %all-reduce.14.cloned.1.call-start = ((), (), s32[]{:S(2)}) async-start(), calls=%async_computation.5 | async-start | bytes 393216
  174.5 116.2 %collective-permute-start.2 = (f32[1,384]{1,0:T(1,128)S(1)}, f32[1,384]{1,0:T(1,128)S(1)}, u32[]{:S(2)}, u32[]{:S(2)}) collective-permute-start(f32[1,384]{1,0:T(1,128)S(1)} %slice.71), channel_id=1, source_target_pairs={{16,0},{32,16},{48,32},{64,48},{80,64},{96,80},{112,96},{128,112},... | collective-permute-start | bytes 4616 | tf_op jit(solution)/shard_map/ppermute | solution.py:15
  291.3 2.5 collective-permute-start.3
  421.3 115.3 %all-to-all-start.2 = ((f32[16,1,3072]{2,1,0:T(1,128)}), f32[16,1,3072]{2,1,0:T(1,128)S(1)}, u32[]{:S(2)}, u32[]{:S(2)}) async-start(f32[16,1,3072]{2,1,0:T(1,128)} %stack.10), calls=%async_computation.2 | async-start | bytes 393216 | tf_op jit(solution)/shard_map/all_to_all | solution.py:74
  427.0 243.9 %all-reduce.16.cloned.1.call-start = ((), (), s32[]{:S(2)}) async-start(), calls=%async_computation.6 | async-start | bytes 393216
  427.1 116.2 %collective-permute-start.4 = (f32[1,384]{1,0:T(1,128)S(1)}, f32[1,384]{1,0:T(1,128)S(1)}, u32[]{:S(2)}, u32[]{:S(2)}) collective-permute-start(f32[1,384]{1,0:T(1,128)S(1)} %slice.75), channel_id=1, source_target_pairs={{16,0},{32,16},{48,32},{64,48},{80,64},{96,80},{112,96},{128,112},... | collective-permute-start | bytes 4616 | tf_op jit(solution)/shard_map/ppermute | solution.py:15
  543.9 2.5 collective-permute-start.5
  558.0 227.4 %collective-permute-start.6 = (f32[1,384]{1,0:T(1,128)S(1)}, f32[1,384]{1,0:T(1,128)S(1)}, u32[]{:S(2)}, u32[]{:S(2)}) collective-permute-start(f32[1,384]{1,0:T(1,128)S(1)} %slice.79), channel_id=1, source_target_pairs={{16,0},{32,16},{48,32},{64,48},{80,64},{96,80},{112,96},{128,112},... | collective-permute-start | bytes 4616 | tf_op jit(solution)/shard_map/ppermute | solution.py:15
  778.8 13.5 %all-to-all-start.3 = ((f32[16,1,3072]{2,1,0:T(1,128)}), f32[16,1,3072]{2,1,0:T(1,128)S(1)}, u32[]{:S(2)}, u32[]{:S(2)}) async-start(f32[16,1,3072]{2,1,0:T(1,128)} %stack.11), calls=%async_computation.3 | async-start | bytes 393216 | tf_op jit(solution)/shard_map/all_to_all | solution.py:74
  785.3 134.1 %all-reduce.18.cloned.1.call-start = ((), (), s32[]{:S(2)}) async-start(), calls=%async_computation.7 | async-start | bytes 393216
  786.0 13.1 %collective-permute-start.7 = (f32[1,384]{1,0:T(1,128)S(1)}, f32[1,384]{1,0:T(1,128)S(1)}, u32[]{:S(2)}, u32[]{:S(2)}) collective-permute-start(f32[1,384]{1,0:T(1,128)S(1)} %slice.80), channel_id=1, source_target_pairs={{0,16},{16,32},{32,48},{48,64},{64,80},{80,96},{96,112},{112,128},... | collective-permute-start | bytes 4616 | tf_op jit(solution)/shard_map/ppermute | solution.py:15
Sparse Core Ops, SparseCore 0:
  46.5 119.2 all-reduce.11
  305.5 112.8 all-reduce.13
  558.1 112.8 all-reduce.15
  810.7 108.6 all-reduce.17
